TPU v7x, 256 devices: a whole 4x4x8 slice. The times are simulated.
256 devices in a mesh: context: 32 (over z, x), ulysses: 4 (over y), dp: 2 (over core).
Axes of the slice: x: 4, y: 4, z: 8, core: 2. Of those that a mesh axis runs over, the one named last changes fastest.
Arguments:
- queries: bfloat16 [32768, 4096], P(('dp', 'context', 'ulysses')), parts along dimension 0, may hold values from -5 to 5
- keys: bfloat16 [32768, 512], P(('dp', 'context', 'ulysses')), parts along dimension 0, may hold values from -5 to 5
- values: bfloat16 [32768, 512], P(('dp', 'context', 'ulysses')), parts along dimension 0, may hold values from -6 to 6
- segments: int32 [32768], P(('dp', 'context')), parts along dimension 0, may hold values from 0 to 63, never falling along the last dimension, each value on 1 to 4096 neighbouring positions
- feat_q: bfloat16 [32, 128, 128], P('ulysses'), may hold values from -2 to 2
- feat_k: bfloat16 [4, 128, 128], P('ulysses'), may hold values from -2 to 2
Outputs:
- error: bfloat16 [32768, 4096], P(('dp', 'context'), 'ulysses'), parts along dimension 0
- grad_keys: bfloat16 [32768, 512], P(('dp', 'context'), 'ulysses'), parts along dimension 0
- grad_feat_q: float32 [64, 128, 128], P(('dp', 'ulysses')), parts along dimension 0
- grad_feat_k: float32 [8, 128, 128], P(('dp', 'ulysses')), parts along dimension 0
There are 2 independent parts, one for each index of `dp`. A program takes and returns all parts, laid end to end along the dimension named above; an argument that names none is the same for every part. Nothing has to cross between parts.
Inputs may be any that keep to these rules, and one draw needn't show every extreme that they name: `segments`: document numbers never fall along the sequence; each document covers 1 to 4096 positions, and one covers exactly 4096.
All inputs are finite; a program needn't handle non-finite values.
Results may differ from a plain program's by a relative error of at most 0.015.
Values may be sent and summed in bfloat16 or wider, within the bound.
A program may use at most 128 MiB of HBM per device.

v0:
```python
import math
import jax
import jax.numpy as jnp
from jax import lax
from jax.sharding import PartitionSpec as P

WIN = 128


def entering(value, axis, join, neutral, backward):
    count, mine = (lax.axis_size(axis), lax.axis_index(axis))
    pieces = jax.tree.map(lambda part: lax.all_gather(part, axis), value)
    if backward:
        pieces = jax.tree.map(lambda part: part[::-1], pieces)
        mine = count - 1 - mine
    so_far = jax.tree.map(
        lambda part, zero: jnp.full_like(part, 0) + jnp.asarray(zero, part.dtype), value, neutral
    )

    def lap(position, so_far):
        longer = join(so_far, jax.tree.map(lambda part: part[position], pieces))
        return jax.tree.map(lambda new, old: jnp.where(position < mine, new, old), longer, so_far)

    return lax.fori_loop(0, count - 1, lap, so_far)


def from_behind(block, axis, distance):
    devices = range(lax.axis_size(axis))
    route = [(i - distance, i) for i in devices if i - distance in devices]
    return lax.ppermute(block, axis, route)


def feature_map(pre):
    return jnp.where(pre > 0, pre + 1.0, jnp.exp(jnp.minimum(pre, 0.0)))


def feature_slope(pre):
    return jnp.where(pre > 0, 1.0, jnp.exp(jnp.minimum(pre, 0.0)))


def join_parts(earlier, later):
    empty_later = later[2] < 0
    keep = (earlier[2] == later[2]) | empty_later
    return (
        later[0] + jnp.where(keep, earlier[0], 0.0),
        later[1] + jnp.where(keep, earlier[1], 0.0),
        jnp.where(empty_later, earlier[2], later[2]),
    )


def widened(form, left, right):
    return jnp.einsum(form, left, right, preferred_element_type=jnp.float32)


def split_pair(whole):
    upper = whole.astype(jnp.bfloat16)
    lower = (whole - upper.astype(jnp.float32)).astype(jnp.bfloat16)
    return (upper, lower)


def paired(form, left, pair, pair_first):
    if pair_first:
        return widened(form, pair[0], left) + widened(form, pair[1], left)
    return widened(form, left, pair[0]) + widened(form, left, pair[1])


def on_device(queries, keys, values, segments, feat_q, feat_k):
    query_all, key_all, value_all = (
        lax.all_to_all(queries, "ulysses", split_axis=1, concat_axis=0, tiled=True),
        lax.all_to_all(keys, "ulysses", split_axis=1, concat_axis=0, tiled=True),
        lax.all_to_all(values, "ulysses", split_axis=1, concat_axis=0, tiled=True),
    )
    length = query_all.shape[0]
    kv_heads, width, feats = feat_k.shape
    group = feat_q.shape[0] // kv_heads
    query_heads = query_all.reshape(length, kv_heads, group, width)
    key_heads = key_all.reshape(length, kv_heads, width)
    value_heads = value_all.reshape(length, kv_heads, width)
    pre_q = widened("rgke,gkef->rgkf", query_heads, feat_q.reshape(kv_heads, group, width, feats))
    phi_q = feature_map(pre_q).astype(jnp.bfloat16)
    pre_k = widened("rge,gef->rgf", key_heads, feat_k)
    phi_k = feature_map(pre_k).astype(jnp.bfloat16)
    here = lax.axis_index("context")
    first_id = segments[0]
    last_id = segments[length - 1]
    tail_k = jnp.where((segments == last_id)[:, None, None], phi_k, jnp.zeros_like(phi_k))
    state_local = widened("rgf,rge->gfe", tail_k, value_heads)
    norm_local = jnp.sum(tail_k.astype(jnp.float32), axis=0)
    blank = (jnp.zeros_like(state_local), jnp.zeros_like(norm_local))
    state_in, norm_in, state_id = entering(
        (state_local, norm_local, last_id),
        "context",
        join_parts,
        (blank[0], blank[1], jnp.int32(-1)),
        False,
    )
    state_parts = split_pair(state_in)
    norm_parts = split_pair(norm_in)
    rim_keys, rim_values, rim_ids = from_behind(
        (key_heads[length - WIN :], value_heads[length - WIN :], segments[length - WIN :]),
        "context",
        1,
    )
    rim_ids = jnp.where(here > 0, rim_ids, -1)
    keys_ext = jnp.concatenate([rim_keys, key_heads], axis=0)
    values_ext = jnp.concatenate([rim_values, value_heads], axis=0)
    ids_ext = jnp.concatenate([rim_ids, segments], axis=0)
    place = jnp.arange(length)
    place_ext = jnp.arange(length + WIN) - WIN
    take_in = segments == state_id
    first_rows = segments == first_id
    inv_scale = 1.0 / math.sqrt(width)
    block = min(512, length)
    cot_state = blank[0]
    cot_norm = blank[1]
    linked = (place[None, :] <= place[:, None]) & (segments[None, :] == segments[:, None])
    linked = linked[:, None, None, :]
    scores = jnp.where(linked, widened("igkf,jgf->igkj", phi_q, phi_k), 0.0)
    carried = take_in[:, None, None]
    numer = widened("igkj,jge->igke", scores.astype(jnp.bfloat16), value_heads) + jnp.where(
        carried[..., None], paired("igkf,gfe->igke", phi_q, state_parts, False), 0.0
    )
    denom = jnp.sum(scores, axis=-1) + jnp.where(
        carried, paired("igkf,gf->igk", phi_q, norm_parts, False), 0.0
    )
    student = numer / denom[..., None]
    seen = (
        (place_ext[None, :] <= place[:, None])
        & (place_ext[None, :] > place[:, None] - WIN)
        & (ids_ext[None, :] == segments[:, None])
    )
    logits = jnp.where(
        seen[:, None, None, :],
        widened("igke,jge->igkj", query_heads, keys_ext) * inv_scale,
        -jnp.inf,
    )
    top = jnp.max(logits, axis=-1, keepdims=True)
    probs = jnp.exp(logits - top)
    teacher = (
        widened("igkj,jge->igke", probs.astype(jnp.bfloat16), values_ext)
        / jnp.sum(probs, axis=-1)[..., None]
    )
    gap = student - teacher
    errors = gap.astype(jnp.bfloat16).reshape(block, kv_heads * group * width)
    upstream = 32.0 * gap
    d_numer = (upstream / denom[..., None]).astype(jnp.bfloat16)
    d_denom = -jnp.sum(upstream * student, axis=-1) / denom
    d_scores = jnp.where(
        linked, widened("igke,jge->igkj", d_numer, value_heads) + d_denom[..., None], 0.0
    ).astype(jnp.bfloat16)
    d_phi_q_parts = widened("igkj,jgf->igkf", d_scores, phi_k) + jnp.where(
        carried[..., None],
        paired("gfe,igke->igkf", d_numer, state_parts, True)
        + d_denom[..., None] * norm_in[None, :, None, :],
        0.0,
    )
    d_phi_k = widened("igkj,igkf->jgf", d_scores, phi_q)
    head_rows = first_rows[:, None, None, None]
    cot_state = widened(
        "igkf,igke->gfe", jnp.where(head_rows, phi_q, jnp.zeros_like(phi_q)), d_numer
    )
    cot_norm = jnp.sum(jnp.where(head_rows, d_denom[..., None] * phi_q, 0.0), axis=(0, 2))
    back_state, back_norm, back_id = entering(
        (cot_state, cot_norm, first_id),
        "context",
        join_parts,
        (blank[0], blank[1], jnp.int32(-1)),
        True,
    )
    take_back = (segments == back_id)[:, None, None]
    back_parts = split_pair(back_state)
    d_phi_k = d_phi_k + jnp.where(
        take_back, paired("gfe,jge->jgf", value_heads, back_parts, True) + back_norm[None], 0.0
    )
    d_pre_k = (d_phi_k * feature_slope(pre_k)).astype(jnp.bfloat16)
    grad_keys = (
        widened("jgf,gef->jge", d_pre_k, feat_k)
        .astype(jnp.bfloat16)
        .reshape(length, kv_heads * width)
    )
    d_pre_q = (d_phi_q_parts * feature_slope(pre_q)).astype(jnp.bfloat16)
    grad_query_maps = widened("rgke,rgkf->gkef", query_heads, d_pre_q).reshape(
        kv_heads * group, width, feats
    )
    grad_key_maps = widened("rge,rgf->gef", key_heads, d_pre_k)
    grad_query_maps, grad_key_maps = (
        lax.psum(grad_query_maps.astype(jnp.bfloat16), "context").astype(jnp.float32),
        lax.psum(grad_key_maps.astype(jnp.bfloat16), "context").astype(jnp.float32),
    )
    scale = 1.0 / math.sqrt(length * lax.axis_size("context"))
    return (errors, grad_keys, grad_query_maps * scale, grad_key_maps * scale)


def solution(mesh):
    in_specs = (
        P(("dp", "context", "ulysses"), None),
        P(("dp", "context", "ulysses"), None),
        P(("dp", "context", "ulysses"), None),
        P(("dp", "context")),
        P("ulysses", None, None),
        P("ulysses", None, None),
    )
    out_specs = (
        P(("dp", "context"), "ulysses"),
        P(("dp", "context"), "ulysses"),
        P(("dp", "ulysses"), None, None),
        P(("dp", "ulysses"), None, None),
    )
    return jax.shard_map(
        on_device, mesh=mesh, in_specs=in_specs, out_specs=out_specs, check_vma=False
    )
```

profile of v0, /device:TPU:8, one launch (start us, length us, event | category | flops | bytes accessed | tf_op | source)
XLA Modules:
  0.0 722.6 jit_solution(18378612023101309730)
XLA Ops:
  9.1 5.4 all-to-all-start
  20.7 4.8 all-to-all-start.2
  27.2 2.8 all-to-all-done.2
  32.0 4.9 all-to-all-start.1
  36.9 2.9 collective-permute-start.1
  40.7 23.7 %all-reduce.2 = (s32[32]{0:T(128)S(1)}, s32[32]{0:T(128)}) all-reduce(s32[32]{0:T(128)S(1)} %get-tuple-element.424, s32[32]{0:T(128)S(1)} %slice_dynamic-update-slice_fusion), channel_id=1, replica_groups=mesh['context'=32,'ulysses'=4,'dp'=2] {'context'}, use_global_device_ids=true, to_apply=%add | all-reduce | flops 64 | bytes 512
  68.4 3.9 collective-permute-start
  72.3 37.9 %all-gather.4 = f32[32,1,128]{2,1,0:T(1,128)S(1)} all-gather(f32[1,1,128]{2,1,0:T(1,128)S(1)} %bitcast.397), channel_id=3, replica_groups=mesh['context'=32,'ulysses'=4,'dp'=2] {'context'}, dimensions={0}, use_global_device_ids=true | all-gather | bytes 16896 | tf_op jit(solution)/shard_map/all_gather | solution.py:12
  112.4 4.0 fusion.10
  118.3 4.0 copy-done.1
  122.3 2.2 fusion.4
  124.5 107.3 %while.36 = (s32[]{:T(128)}, f32[1,128,128]{2,1,0:T(8,128)S(1)}, f32[1,128]{1,0:T(1,128)S(1)}, s32[]{:T(128)}, s32[]{:T(128)}, /*index=5*/f32[32,1,128,128]{3,2,...) while((s32[]{:T(128)}, f32[1,128,128]{2,1,0:T(8,128)S(1)}, ...), condition=%wide.region_2.3_spmd.clone, body=%wide.region_1.2_spmd.clone.sunk | while | flops 66057 | bytes 198336 | solution.py:24
  238.4 2.4 copy.112
  242.2 4.7 fusion.24
  248.2 4.8 multiply_reduce_fusion
  256.5 2.1 fusion.84
  259.1 5.2 fusion.39
  266.0 37.3 %all-gather.5 = f32[32,1,128]{2,1,0:T(1,128)S(1)} all-gather(f32[1,1,128]{2,1,0:T(1,128)S(1)} %bitcast.396), channel_id=5, replica_groups=mesh['context'=32,'ulysses'=4,'dp'=2] {'context'}, dimensions={0}, use_global_device_ids=true | all-gather | bytes 16896 | tf_op jit(solution)/shard_map/all_gather | solution.py:12
  303.3 2.3 copy.100
  305.6 101.9 %all-reduce.5.cloned.1.call-done = bf16[8,128,128]{1,2,0:T(8,128)(2,1)} async-done(((bf16[8,128,128]{1,2,0:T(8,128)(2,1)}), bf16[8,128,128]{1,2,0:T(8,128)(2,1)}) %all-reduce.5.cloned.1.call-update) | async-done | bytes 262160 | tf_op jit(solution)/shard_map/psum | solution.py:187
  409.4 76.1 %all-gather.11.cloned.1.call-done = f32[4096,128]{1,0:T(8,128)} async-done(((f32[128,128]{1,0:T(8,128)}), f32[4096,128]{1,0:T(8,128)}) %all-gather.11.cloned.1.call-update) | async-done | bytes 2097168 | tf_op jit(solution)/shard_map/all_gather | solution.py:12
  487.3 81.0 %while.37 = (s32[]{:T(128)}, f32[1,128,128]{2,1,0:T(8,128)S(1)}, f32[1,128]{1,0:T(1,128)S(1)}, s32[]{:T(128)}, s32[]{:T(128)}, /*index=5*/f32[32,1,128,128]{3,2,...) while((s32[]{:T(128)}, f32[1,128,128]{2,1,0:T(8,128)S(1)}, ...), condition=%wide.region_9.10_spmd.clone, body=%wide.region_8.9_spmd.clone.sunk | while | flops 66057 | bytes 198336 | solution.py:24
  570.5 3.7 fusion.41
  575.3 140.0 %psum.15 = bf16[1,128,128]{1,2,0:T(8,128)(2,1)S(1)} all-reduce(bf16[1,128,128]{1,2,0:T(8,128)(2,1)S(1)} %fusion.42), channel_id=1, replica_groups=mesh['context'=32,'ulysses'=4,'dp'=2] {'context'}, use_global_device_ids=true, to_apply=%region_11.12 | all-reduce | flops 16384 | bytes 65536 | tf_op jit(solution)/shard_map/psum | solution.py:188
  (304 shorter events, 108.0 us)
Async XLA Ops:
  7.2 103.3 %copy-start = (bf16[8,128,128]{2,1,0:T(8,128)(2,1)S(1)}, bf16[8,128,128]{2,1,0:T(8,128)(2,1)}, u32[]{:S(2)}) copy-start(bf16[8,128,128]{2,1,0:T(8,128)(2,1)} %param.14) | copy-start | bytes 786436
  7.2 23.7 %copy-start.13 = (bf16[128,4096]{1,0:T(8,128)(2,1)S(1)}, bf16[128,4096]{1,0:T(8,128)(2,1)}, u32[]{:S(2)}) copy-start(bf16[128,4096]{1,0:T(8,128)(2,1)} %param.10) | copy-start | bytes 3145732
  9.1 11.6 %all-to-all-start = ((bf16[128,4,128]{2,0,1:T(8,128)(2,1)}), bf16[128,4,128]{2,0,1:T(8,128)(2,1)S(1)}, u32[]{:S(2)}, u32[]{:S(2)}) async-start(bf16[128,4,128]{2,0,1:T(8,128)(2,1)} %copy.71), calls=%async_computation | async-start | bytes 262144 | tf_op jit(solution)/shard_map/all_to_all | solution.py:70
  20.7 95.7 %copy-start.11 = (bf16[128,4,128]{2,0,1:T(8,128)(2,1)}, bf16[128,4,128]{2,0,1:T(8,128)(2,1)S(1)}, u32[]{:S(2)}) copy-start(bf16[128,4,128]{2,0,1:T(8,128)(2,1)S(1)} %all-to-all-done) | copy-start | bytes 393220
  20.7 9.3 %all-to-all-start.2 = ((bf16[128,4,128]{0,2,1:T(8,128)(2,1)}), bf16[128,4,128]{0,2,1:T(8,128)(2,1)S(1)}, u32[]{:S(2)}, u32[]{:S(2)}) async-start(bf16[128,4,128]{0,2,1:T(8,128)(2,1)} %bitcast.15), calls=%async_computation.2 | async-start | bytes 262144 | tf_op jit(solution)/shard_map/all_to_all | solution.py:71
  25.5 98.9 %all-gather.9.cloned.1.call-start = ((), (), s32[]{:S(2)}) async-start(), calls=%async_computation.4 | async-start | bytes 2162688 | tf_op jit(solution)/shard_map/all_gather | solution.py:12
  27.2 85.2 %copy-start.16 = (bf16[128,512]{1,0:T(8,128)(2,1)}, bf16[128,512]{1,0:T(8,128)(2,1)S(1)}, u32[]{:S(2)}) copy-start(bf16[128,512]{1,0:T(8,128)(2,1)S(1)} %get-tuple-element.417) | copy-start | bytes 393220
  30.0 37.7 %copy-start.9 = (bf16[128,4,128]{0,2,1:T(8,128)(2,1)}, bf16[128,4,128]{0,2,1:T(8,128)(2,1)S(1)}, u32[]{:S(2)}) copy-start(bf16[128,4,128]{0,2,1:T(8,128)(2,1)S(1)} %all-to-all-done.2) | copy-start | bytes 393220
  30.9 6.0 copy-start.19
  32.0 78.2 %all-to-all-start.1 = ((bf16[128,4,1024]{2,0,1:T(8,128)(2,1)}), bf16[128,4,1024]{2,0,1:T(8,128)(2,1)S(1)}, u32[]{:S(2)}, u32[]{:S(2)}) async-start(bf16[128,4,1024]{2,0,1:T(8,128)(2,1)} %bitcast.364), calls=%async_computation.1 | async-start | bytes 2097152 | tf_op jit(solution)/shard_map/all_to_all | solution.py:69
  36.9 370.5 %all-reduce.5.cloned.1.call-start = ((), (), s32[]{:S(2)}) async-start(), calls=%async_computation.3 | async-start | bytes 524288 | tf_op jit(solution)/shard_map/psum | solution.py:187
  36.9 27.5 %collective-permute-start.1 = (s32[128]{0:T(128)S(1)}, s32[128]{0:T(128)S(1)}, u32[]{:S(2)}, u32[]{:S(2)}) collective-permute-start(s32[128]{0:T(128)S(1)} %slice.24), channel_id=1, source_target_pairs={{0,8},{8,16},{16,24},{24,32},{32,40},{40,48},{48,56},{56,64},{64,7... | collective-permute-start | bytes 1544 | tf_op jit(solution)/shard_map/ppermute | solution.py:30
  40.7 71.7 %copy-start.14 = (pred[512,512]{0,1:T(8,128)(4,1)}, pred[512,512]{0,1:T(8,128)(4,1)S(1)}, u32[]{:S(2)}) copy-start(pred[512,512]{0,1:T(8,128)(4,1)S(1)} %fusion.66) | copy-start | bytes 786436
  64.8 53.4 %copy-start.7 = (pred[512,640]{0,1:T(8,128)(4,1)}, pred[512,640]{0,1:T(8,128)(4,1)S(1)}, u32[]{:S(2)}) copy-start(pred[512,640]{0,1:T(8,128)(4,1)S(1)} %fusion.31) | copy-start | bytes 983044
  66.4 50.1 %collective-permute-start.2 = (bf16[128,1,128]{2,0,1:T(8,128)(2,1)S(1)}, bf16[128,1,128]{2,0,1:T(8,128)(2,1)S(1)}, u32[]{:S(2)}, u32[]{:S(2)}) collective-permute-start(bf16[128,1,128]{2,0,1:T(8,128)(2,1)S(1)} %slice_bitcast_fusion), channel_id=1, source_target_pairs={{0,8},{8,16},{16,24},{24,32},{32,40},{40,48},{48,56},{56,64},{64,7... | collective-permute-start | bytes 98312 | tf_op jit(solution)/shard_map/ppermute | solution.py:30
  68.4 178.5 %collective-permute-start = (bf16[128,1,128]{0,2,1:T(8,128)(2,1)}, bf16[128,1,128]{0,2,1:T(8,128)(2,1)}, u32[]{:S(2)}, u32[]{:S(2)}) collective-permute-start(bf16[128,1,128]{0,2,1:T(8,128)(2,1)} %slice_bitcast_fusion.1), channel_id=1, source_target_pairs={{0,8},{8,16},{16,24},{24,32},{32,40},{40,48},{48,56},{56,64},{64,7... | collective-permute-start | bytes 98312 | tf_op jit(solution)/shard_map/ppermute | solution.py:30
  110.4 6.1 copy-start.2
  238.4 8.5 %slice-start = ((s8[10485760]{0:T(1024)(128)(4,1)}), s8[2097152]{0:T(1024)(128)(4,1)S(1)}, s32[]{:S(2)}) async-start(s8[10485760]{0:T(1024)(128)(4,1)} %bitcast.377), calls=%async_computation.6 | async-start | bytes 4194304
  242.1 4.8 slice-start.1
  242.1 6.0 slice-start.2
  242.1 6.0 copy-start.8
  242.1 6.0 copy-start.18
  259.1 5.3 copy-start.6
  264.3 221.2 %all-gather.11.cloned.1.call-start = ((), (), s32[]{:S(2)}) async-start(), calls=%async_computation.5 | async-start | bytes 2162688 | tf_op jit(solution)/shard_map/all_gather | solution.py:12
  (10 other events, 26.8 us)
Sparse Core Ops, SparseCore 0:
  31.0 79.2 all-gather.8
  264.4 142.9 all-reduce.4
  410.6 74.8 all-gather.10
where the time goes:
time: 727 us; the launch traced here: 723 us
  blocking collectives  239 us (33%)
  waiting for transfers between devices  181 us (25%)
  loops' own time  123 us (17%)
  local copies, waits for them, and re-layouts  61.8 us (9%)
  matrix products  44.6 us (6%)
  other arithmetic  35.4 us (5%)
  starting transfers between devices  23.4 us (3%)
  between operations  14.2 us (2%)
    psum x1, blocking collectives, on_device(): lax.psum(grad_key_maps.astype(jnp.bfloat16), 'context').astype(jnp.float32)  140 us
    another operation x2, loops' own time, entering(): return lax.fori_loop(0, count - 1, lap, so_far)  123 us
    psum x1, waiting for transfers between devices, on_device(): lax.psum(grad_query_maps.astype(jnp.bfloat16), 'context')  102 us
    all_gather x2, waiting for transfers between devices, entering(): pieces = jax.tree.map(lambda part: lax.all_gather(part, axis), value)  76.1 us
    all_gather x2, blocking collectives, entering(): pieces = jax.tree.map(lambda part: lax.all_gather(part, axis), value)  75.2 us
    dot_general x21, matrix products, widened(): return jnp.einsum(form, left, right, preferred_element_type=jnp.float32)  44.6 us
    dynamic_slice x62, local copies, waits for them, and re-layouts, lap(): longer = join(so_far, jax.tree.map(lambda part: part[position], pieces))  36.4 us
    select_n x124, other arithmetic, lap(): jnp.where(position < mine, new, old)  28.5 us
  transfers between devices with their start and end apart: 9, of which 3 were waited for; matrix products, arithmetic and copies ran while one was open for 12% of the time, Pallas kernels for 0%

commit v1 on v0

--- a/solution.py
+++ b/solution.py
@@ -184,7 +184,9 @@
     )
     grad_key_maps = widened("rge,rgf->gef", key_heads, d_pre_k)
     grad_query_maps, grad_key_maps = (
-        lax.psum(grad_query_maps.astype(jnp.bfloat16), "context").astype(jnp.float32),
+        jnp.sum(lax.all_gather(grad_query_maps.astype(jnp.bfloat16), "context"), axis=0).astype(
+            jnp.float32
+        ),
         lax.psum(grad_key_maps.astype(jnp.bfloat16), "context").astype(jnp.float32),
     )
     scale = 1.0 / math.sqrt(length * lax.axis_size("context"))

time: 727 us -> 580 us (0.80)
  waiting for transfers between devices: 181 us -> 26.1 us
    psum x1 -> x0, waiting for transfers between devices: 102 us -> none  [on_device(): lax.psum(grad_query_maps.astype(jnp.bfloat16), 'context')]
    all_gather x2, waiting for transfers between devices: 76.1 us -> 23.2 us  [entering(): pieces = jax.tree.map(lambda part: lax.all_gather(part, axis), value)]
    unnamed x60 -> x51, local copies, waits for them, and re-layouts: 14.8 us -> 12.7 us
  transfers between devices with their start and end apart: 9 -> 9, of which waited for: 3 -> 2; matrix products, arithmetic and copies ran while one was open for 12% -> 22% of each run, Pallas kernels for 0% -> 0%
where the time goes in v1:
time: 580 us; the launch traced here: 576 us
  blocking collectives  239 us (41%)
  loops' own time  124 us (21%)
  local copies, waits for them, and re-layouts  61.9 us (11%)
  matrix products  49.3 us (8%)
  other arithmetic  39.1 us (7%)
  waiting for transfers between devices  26.1 us (4%)
  starting transfers between devices  23.2 us (4%)
  between operations  14.2 us (2%)
    psum x1, blocking collectives, on_device(): lax.psum(grad_key_maps.astype(jnp.bfloat16), 'context').astype(jnp.float32)  140 us
    another operation x2, loops' own time, entering(): return lax.fori_loop(0, count - 1, lap, so_far)  124 us
    all_gather x2, blocking collectives, entering(): pieces = jax.tree.map(lambda part: lax.all_gather(part, axis), value)  75.3 us
    dot_general x21, matrix products, widened(): return jnp.einsum(form, left, right, preferred_element_type=jnp.float32)  49.3 us
    dynamic_slice x62, local copies, waits for them, and re-layouts, lap(): longer = join(so_far, jax.tree.map(lambda part: part[position], pieces))  36.4 us
    select_n x124, other arithmetic, lap(): jnp.where(position < mine, new, old)  28.4 us
    unnamed x1, blocking collectives  23.6 us
    all_gather x2, waiting for transfers between devices, entering(): pieces = jax.tree.map(lambda part: lax.all_gather(part, axis), value)  23.2 us
  transfers between devices with their start and end apart: 9, of which 2 were waited for; matrix products, arithmetic and copies ran while one was open for 22% of the time, Pallas kernels for 0%

profile of v1, /device:TPU:8, one launch (start us, length us, event | category | flops | bytes accessed | tf_op | source)
XLA Modules:
  0.0 576.4 jit_solution(139579222113430922)
XLA Ops:
  9.1 5.4 all-to-all-start
  20.8 4.8 all-to-all-start.2
  27.3 2.8 all-to-all-done.2
  32.1 4.9 all-to-all-start.1
  37.0 2.9 collective-permute-start.1
  40.9 23.6 %all-reduce.2 = (s32[32]{0:T(128)S(1)}, s32[32]{0:T(128)}) all-reduce(s32[32]{0:T(128)S(1)} %get-tuple-element.424, s32[32]{0:T(128)S(1)} %slice_dynamic-update-slice_fusion), channel_id=1, replica_groups=mesh['context'=32,'ulysses'=4,'dp'=2] {'context'}, use_global_device_ids=true, to_apply=%add | all-reduce | flops 64 | bytes 512
  67.2 3.8 collective-permute-start
  71.0 38.0 %all-gather.5 = f32[32,1,128]{2,1,0:T(1,128)S(1)} all-gather(f32[1,1,128]{2,1,0:T(1,128)S(1)} %bitcast.397), channel_id=3, replica_groups=mesh['context'=32,'ulysses'=4,'dp'=2] {'context'}, dimensions={0}, use_global_device_ids=true | all-gather | bytes 16896 | tf_op jit(solution)/shard_map/all_gather | solution.py:12
  111.3 4.0 fusion.10
  117.2 4.0 copy-done.1
  121.2 2.2 fusion.4
  123.4 107.2 %while.36 = (s32[]{:T(128)}, f32[1,128,128]{2,1,0:T(8,128)S(1)}, f32[1,128]{1,0:T(1,128)S(1)}, s32[]{:T(128)}, s32[]{:T(128)}, /*index=5*/f32[32,1,128,128]{3,2,...) while((s32[]{:T(128)}, f32[1,128,128]{2,1,0:T(8,128)S(1)}, ...), condition=%wide.region_2.3_spmd.clone, body=%wide.region_1.2_spmd.clone.sunk | while | flops 66057 | bytes 198336 | solution.py:24
  237.9 2.2 copy.111
  240.1 2.2 copy.112
  243.0 4.5 fusion.24
  247.5 8.3 %multiply_reduce_fusion = (f32[512,8]{0,1:T(8,128)S(1)}, bf16[512,1,8,128]{0,3,2,1:T(8,128)(2,1)S(1)}, bf16[512,1,8,128]{0,3,2,1:T(8,128)(2,1)}) fusion(f32[512,1,8,128]{0,3,2,1:T(8,128)S(1)} %fusion.24, f32[512,8]{0,1:T(8,128)S(1)} %fusion.105, f32[512,8]{0,1:T(8,128)S(1)} %fusion.4, f32[640,512,8]{1,0,2:T(8,128)} %copy-done.1, ...), kind=kOutput, calls=%fused_computation.42 | convolution fusion | flops 686092288 | bytes 15237120 | tf_op jit(solution)/shard_map/igkj,jge->igke/dot_general | solution.py:52
  260.5 2.5 fusion.84
  263.1 4.8 fusion.39
  270.3 37.3 %all-gather.6 = f32[32,1,128]{2,1,0:T(1,128)S(1)} all-gather(f32[1,1,128]{2,1,0:T(1,128)S(1)} %bitcast.396), channel_id=5, replica_groups=mesh['context'=32,'ulysses'=4,'dp'=2] {'context'}, dimensions={0}, use_global_device_ids=true | all-gather | bytes 16896 | tf_op jit(solution)/shard_map/all_gather | solution.py:12
  309.2 23.2 %all-gather.13.cloned.1.call-done = f32[4096,128]{1,0:T(8,128)} async-done(((f32[128,128]{1,0:T(8,128)}), f32[4096,128]{1,0:T(8,128)}) %all-gather.13.cloned.1.call-update) | async-done | bytes 2097168 | tf_op jit(solution)/shard_map/all_gather | solution.py:12
  334.1 81.1 %while.37 = (s32[]{:T(128)}, f32[1,128,128]{2,1,0:T(8,128)S(1)}, f32[1,128]{1,0:T(1,128)S(1)}, s32[]{:T(128)}, s32[]{:T(128)}, /*index=5*/f32[32,1,128,128]{3,2,...) while((s32[]{:T(128)}, f32[1,128,128]{2,1,0:T(8,128)S(1)}, ...), condition=%wide.region_9.10_spmd.clone, body=%wide.region_8.9_spmd.clone.sunk | while | flops 66057 | bytes 198336 | solution.py:24
  417.5 3.7 fusion.41
  421.4 140.1 %psum.7 = bf16[1,128,128]{1,2,0:T(8,128)(2,1)S(1)} all-reduce(bf16[1,128,128]{1,2,0:T(8,128)(2,1)S(1)} %fusion.42), channel_id=1, replica_groups=mesh['context'=32,'ulysses'=4,'dp'=2] {'context'}, use_global_device_ids=true, to_apply=%region_11.12 | all-reduce | flops 16384 | bytes 65536 | tf_op jit(solution)/shard_map/psum | solution.py:190
  563.1 5.5 reduce_sum.62
  (296 shorter events, 107.8 us)
Async XLA Ops:
  7.2 102.1 %copy-start = (bf16[8,128,128]{2,1,0:T(8,128)(2,1)S(1)}, bf16[8,128,128]{2,1,0:T(8,128)(2,1)}, u32[]{:S(2)}) copy-start(bf16[8,128,128]{2,1,0:T(8,128)(2,1)} %param.14) | copy-start | bytes 786436
  7.2 23.8 %copy-start.9 = (bf16[128,4096]{1,0:T(8,128)(2,1)S(1)}, bf16[128,4096]{1,0:T(8,128)(2,1)}, u32[]{:S(2)}) copy-start(bf16[128,4096]{1,0:T(8,128)(2,1)} %param.10) | copy-start | bytes 3145732
  9.1 11.7 %all-to-all-start = ((bf16[128,4,128]{2,0,1:T(8,128)(2,1)}), bf16[128,4,128]{2,0,1:T(8,128)(2,1)S(1)}, u32[]{:S(2)}, u32[]{:S(2)}) async-start(bf16[128,4,128]{2,0,1:T(8,128)(2,1)} %copy.69), calls=%async_computation | async-start | bytes 262144 | tf_op jit(solution)/shard_map/all_to_all | solution.py:70
  20.8 94.6 %copy-start.7 = (bf16[128,4,128]{2,0,1:T(8,128)(2,1)}, bf16[128,4,128]{2,0,1:T(8,128)(2,1)S(1)}, u32[]{:S(2)}) copy-start(bf16[128,4,128]{2,0,1:T(8,128)(2,1)S(1)} %all-to-all-done) | copy-start | bytes 393220
  20.8 9.3 %all-to-all-start.2 = ((bf16[128,4,128]{0,2,1:T(8,128)(2,1)}), bf16[128,4,128]{0,2,1:T(8,128)(2,1)S(1)}, u32[]{:S(2)}, u32[]{:S(2)}) async-start(bf16[128,4,128]{0,2,1:T(8,128)(2,1)} %bitcast.15), calls=%async_computation.2 | async-start | bytes 262144 | tf_op jit(solution)/shard_map/all_to_all | solution.py:71
  25.6 97.8 %all-gather.11.cloned.1.call-start = ((), (), s32[]{:S(2)}) async-start(), calls=%async_computation.3 | async-start | bytes 2162688 | tf_op jit(solution)/shard_map/all_gather | solution.py:12
  27.3 84.0 %copy-start.13 = (bf16[128,512]{1,0:T(8,128)(2,1)}, bf16[128,512]{1,0:T(8,128)(2,1)S(1)}, u32[]{:S(2)}) copy-start(bf16[128,512]{1,0:T(8,128)(2,1)S(1)} %get-tuple-element.417) | copy-start | bytes 393220
  30.1 37.1 %copy-start.5 = (bf16[128,4,128]{0,2,1:T(8,128)(2,1)}, bf16[128,4,128]{0,2,1:T(8,128)(2,1)S(1)}, u32[]{:S(2)}) copy-start(bf16[128,4,128]{0,2,1:T(8,128)(2,1)S(1)} %all-to-all-done.2) | copy-start | bytes 393220
  31.0 6.0 %copy-start.16 = (s32[512]{0:T(512)S(1)}, s32[512]{0:T(512)}, u32[]{:S(2)}) copy-start(s32[512]{0:T(512)} %param.13) | copy-start | bytes 6148
  32.1 77.0 %all-to-all-start.1 = ((bf16[128,4,1024]{2,0,1:T(8,128)(2,1)}), bf16[128,4,1024]{2,0,1:T(8,128)(2,1)S(1)}, u32[]{:S(2)}, u32[]{:S(2)}) async-start(bf16[128,4,1024]{2,0,1:T(8,128)(2,1)} %bitcast.365), calls=%async_computation.1 | async-start | bytes 2097152 | tf_op jit(solution)/shard_map/all_to_all | solution.py:69
  37.0 295.4 %all-gather.13.cloned.1.call-start = ((), (), s32[]{:S(2)}) async-start(), calls=%async_computation.4 | async-start | bytes 2162688 | tf_op jit(solution)/shard_map/all_gather | solution.py:12
  37.0 27.5 %collective-permute-start.1 = (s32[128]{0:T(128)S(1)}, s32[128]{0:T(128)S(1)}, u32[]{:S(2)}, u32[]{:S(2)}) collective-permute-start(s32[128]{0:T(128)S(1)} %slice.24), channel_id=1, source_target_pairs={{0,8},{8,16},{16,24},{24,32},{32,40},{40,48},{48,56},{56,64},{64,7... | collective-permute-start | bytes 1544 | tf_op jit(solution)/shard_map/ppermute | solution.py:30
  40.9 202.1 %copy-start.11 = (pred[512,512]{0,1:T(8,128)(4,1)}, pred[512,512]{0,1:T(8,128)(4,1)S(1)}, u32[]{:S(2)}) copy-start(pred[512,512]{0,1:T(8,128)(4,1)S(1)} %fusion.66) | copy-start | bytes 786436
  64.9 52.3 %copy-start.3 = (pred[512,640]{0,1:T(8,128)(4,1)}, pred[512,640]{0,1:T(8,128)(4,1)S(1)}, u32[]{:S(2)}) copy-start(pred[512,640]{0,1:T(8,128)(4,1)S(1)} %fusion.31) | copy-start | bytes 983044
  65.8 49.5 %collective-permute-start.2 = (bf16[128,1,128]{2,0,1:T(8,128)(2,1)S(1)}, bf16[128,1,128]{2,0,1:T(8,128)(2,1)S(1)}, u32[]{:S(2)}, u32[]{:S(2)}) collective-permute-start(bf16[128,1,128]{2,0,1:T(8,128)(2,1)S(1)} %slice_bitcast_fusion), channel_id=1, source_target_pairs={{0,8},{8,16},{16,24},{24,32},{32,40},{40,48},{48,56},{56,64},{64,7... | collective-permute-start | bytes 98312 | tf_op jit(solution)/shard_map/ppermute | solution.py:30
  67.2 180.2 %collective-permute-start = (bf16[128,1,128]{0,2,1:T(8,128)(2,1)S(1)}, bf16[128,1,128]{0,2,1:T(8,128)(2,1)}, u32[]{:S(2)}, u32[]{:S(2)}) collective-permute-start(bf16[128,1,128]{0,2,1:T(8,128)(2,1)S(1)} %slice_bitcast_fusion.1), channel_id=1, source_target_pairs={{0,8},{8,16},{16,24},{24,32},{32,40},{40,48},{48,56},{56,64},{64,7... | collective-permute-start | bytes 98312 | tf_op jit(solution)/shard_map/ppermute | solution.py:30
  117.2 4.0 copy-start.1
  237.9 5.0 copy-start.18
  243.0 4.5 copy-start.4
  243.0 4.5 copy-start.15
  256.9 306.2 %all-gather.15.cloned.1.call-start = ((), (), s32[]{:S(2)}) async-start(), calls=%async_computation.5 | async-start | bytes 8650752 | tf_op jit(solution)/shard_map/all_gather | solution.py:187
  263.1 6.7 %copy-start.19 = (s32[32]{0:T(128)S(1)}, s32[32]{0:T(128)}, u32[]{:S(2)}) copy-start(s32[32]{0:T(128)} %get-tuple-element.415) | copy-start | bytes 388
  267.9 39.7 %copy-start.10 = (bf16[512,1,8,128]{0,3,2,1:T(8,128)(2,1)S(1)}, bf16[512,1,8,128]{0,3,2,1:T(8,128)(2,1)}, u32[]{:S(2)}) copy-start(bf16[512,1,8,128]{0,3,2,1:T(8,128)(2,1)} %get-tuple-element.420) | copy-start | bytes 3145732
  417.4 144.8 %copy-start.17 = (bf16[1,128,128]{2,1,0:T(8,128)(2,1)S(1)}, bf16[1,128,128]{2,1,0:T(8,128)(2,1)}, u32[]{:S(2)}) copy-start(bf16[1,128,128]{2,1,0:T(8,128)(2,1)} %param.15) | copy-start | bytes 98308
  (5 other events, 11.7 us)
Sparse Core Ops, SparseCore 0:
  31.1 79.4 all-gather.10
  257.1 75.2 all-gather.12
  335.0 95.0 all-gather.14
